TPU v7x, 32 devices: a whole 2x2x4 slice. The times are simulated.
32 devices in a mesh: group: 2 (over x), src: 16 (over z, y, core).
Axes of the slice: x: 2, y: 2, z: 4, core: 2. Of those that a mesh axis runs over, the one named last changes fastest.
Arguments:
- rcv_points: float32 [3, 4096], P(None, ('group', 'src')), parts along dimension 1, may hold values from -1 to 1
- rcv_normals: float32 [3, 4096], P(None, ('group', 'src')), parts along dimension 1, may hold values from -4 to 4
- left_modes: float32 [8, 4096], P(None, ('group', 'src')), parts along dimension 1, may hold values from -5 to 5
- vertices: float32 [3, 2048], P(None, ('group', 'src')), parts along dimension 1, may hold values from -1 to 1
- connect: int32 [2, 4096], P(None, ('group', 'src')), parts along dimension 1, may hold values from 0 to 1023, as said below
- right_modes: float32 [8, 4096], P(None, ('group', 'src')), parts along dimension 1, may hold values from -0.125 to 0.125
- mode_weights: float32 [16], P('group'), parts along dimension 0, may hold values from 0.25 to 1
Outputs:
- rcv_grad: float32 [6, 4096], P(None, ('group', 'src')), parts along dimension 1
- vert_grad: float32 [3, 2048], P(None, ('group', 'src')), parts along dimension 1
There are 2 independent parts, one for each index of `group`. A program takes and returns all parts, laid end to end along the dimension named above; each array names one. Nothing has to cross between parts.
Inputs may be any that keep to these rules, and one draw needn't show every extreme that they name: `connect`: a panel's first vertex is one of the 64 vertices held at the same index of src as the panel, and its second vertex is the next vertex number.
All inputs are finite; a program needn't handle non-finite values.
Results may differ from a plain program's by a relative error of at most 0.0003.
Values sent between devices are 32-bit elements; how exact they have to be, the bound alone decides.
No kernel may reach another device: no remote copies, remote signals or barrier semaphores. Data moves between devices by JAX's collectives and lax.ppermute only.
A program may use at most 64 MiB of HBM per device.

v0:
```python
import math
import jax
import jax.numpy as jnp
from jax import lax
from jax.sharding import PartitionSpec as P

core_term = 0.05
inverse_four_pi = 0.25 / math.pi


def shifted(value, axis, steps):
    count = lax.axis_size(axis)
    leading, last = (max(0, -steps), min(count, count - steps))
    return lax.ppermute(value, axis, [(source, source + steps) for source in range(leading, last)])


def lift_points(raw):
    return jnp.stack([raw[0], raw[1], 0.5 + 0.2 * raw[2]])


def place_points(raw):
    return jnp.stack([raw[0], raw[1], 0.2 * raw[2]])


def tile_energy(points, normals, first_end, second_end, coefficient):
    rel_first = points[:, None, :] - first_end[:, :, None]
    rel_second = points[:, None, :] - second_end[:, :, None]
    segment = (second_end - first_end)[:, :, None]
    cross_x = rel_first[1] * rel_second[2] - rel_first[2] * rel_second[1]
    cross_y = rel_first[2] * rel_second[0] - rel_first[0] * rel_second[2]
    cross_z = rel_first[0] * rel_second[1] - rel_first[1] * rel_second[0]
    cross_sq = cross_x * cross_x + cross_y * cross_y + cross_z * cross_z
    dist_first = jnp.sqrt(jnp.sum(rel_first * rel_first, axis=0))
    dist_second = jnp.sqrt(jnp.sum(rel_second * rel_second, axis=0))
    along_term = jnp.sum(segment * (rel_first / dist_first - rel_second / dist_second), axis=0)
    span_sq = jnp.sum(segment * segment, axis=0)
    denominator = cross_sq + core_term * (span_sq + 1.0)
    normal_term = (
        normals[0][None, :] * cross_x
        + normals[1][None, :] * cross_y
        + normals[2][None, :] * cross_z
    )
    influence = inverse_four_pi * normal_term * along_term / denominator
    return jnp.sum(coefficient * influence)


def tile_gradients(points, normals, first_end, second_end, coefficient):
    return jax.grad(tile_energy, argnums=(0, 1, 2, 3))(
        points, normals, first_end, second_end, coefficient
    )


def on_device(rcv_points, rcv_normals, left_modes, vertices, connect, right_modes, mode_weights):
    own_count = vertices.shape[1]
    next_first = shifted(vertices[:, :1], "src", -1)
    extended = jnp.concatenate([vertices, next_first], axis=1)
    places = place_points(extended)
    base_vertex = lax.axis_index("src") * own_count
    local_first = connect[0] - base_vertex
    local_second = local_first + 1
    first_end = places[:, local_first]
    second_end = places[:, local_second]
    points = lift_points(rcv_points)
    chain_scale = jnp.array([1.0, 1.0, 0.2], dtype=jnp.float32)[:, None]
    weighted = right_modes * mode_weights[:, None]
    receiver_count = rcv_points.shape[1] * lax.axis_size("src")
    source_count = connect.shape[1]
    start_totals = (
        jnp.zeros((3, source_count), jnp.float32),
        jnp.zeros((3, source_count), jnp.float32),
        jnp.zeros((6, receiver_count), jnp.float32),
    )
    shard_points = lax.all_gather(points, "src", axis=1, tiled=True)
    shard_normals = lax.all_gather(rcv_normals, "src", axis=1, tiled=True)
    shard_left = lax.all_gather(left_modes, "src", axis=1, tiled=True)
    row_count = shard_points.shape[1]
    width_rows = math.gcd(row_count, 2048)

    def advance(number, inner):
        sum_first, sum_second, receiver_buffer = inner
        local_start = number * width_rows
        block_points = lax.dynamic_slice_in_dim(shard_points, local_start, width_rows, 1)
        block_normals = lax.dynamic_slice_in_dim(shard_normals, local_start, width_rows, 1)
        block_left = lax.dynamic_slice_in_dim(shard_left, local_start, width_rows, 1)
        coefficient = jnp.einsum("mj,mi->ji", weighted, block_left, precision=lax.Precision.HIGHEST)
        grads = tile_gradients(block_points, block_normals, first_end, second_end, coefficient)
        rows_out = jnp.concatenate([grads[0] * chain_scale, grads[1]], axis=0)
        receiver_buffer = lax.dynamic_update_slice_in_dim(receiver_buffer, rows_out, local_start, 1)
        return (sum_first + grads[2], sum_second + grads[3], receiver_buffer)

    sum_first, sum_second, receiver_buffer = lax.fori_loop(
        0, row_count // width_rows, advance, start_totals
    )
    rcv_grad = lax.psum_scatter(receiver_buffer, "src", scatter_dimension=1, tiled=True)
    vertex_partial = jnp.zeros((3, own_count + 1), jnp.float32)
    vertex_partial = (
        vertex_partial.at[:, local_first].add(sum_first).at[:, local_second].add(sum_second)
    )
    incoming = shifted(vertex_partial[:, own_count:], "src", 1)
    own_part = vertex_partial[:, :own_count]
    own_part = jnp.concatenate([own_part[:, :1] + incoming, own_part[:, 1:]], axis=1)
    vert_grad = own_part * chain_scale
    return (rcv_grad, vert_grad)


def solution(mesh):
    in_specs = (
        P(None, ("group", "src")),
        P(None, ("group", "src")),
        P(None, ("group", "src")),
        P(None, ("group", "src")),
        P(None, ("group", "src")),
        P(None, ("group", "src")),
        P("group"),
    )
    out_specs = (P(None, ("group", "src")), P(None, ("group", "src")))
    return jax.shard_map(
        on_device, mesh=mesh, in_specs=in_specs, out_specs=out_specs, check_vma=False
    )
```

profile of v0, /device:TPU:0, one launch (start us, length us, event | category | flops | bytes accessed | tf_op | source)
XLA Modules:
  0.0 154.4 jit_solution(849035136935577808)
XLA Ops:
  7.2 0.0 reduce-scatter.2.cloned.1.call-start
  7.2 1.3 collective-permute-start
  8.5 0.7 multiply_add_fusion.1
  9.2 0.7 slice.81
  9.9 23.8 %all_gather.10 = f32[3,2048]{1,0:T(4,128)S(1)} all-gather(f32[3,128]{1,0:T(4,128)S(1)} %pad_maximum_fusion.3), channel_id=1, replica_groups=mesh['group'=2,'src'=16] {'src'}, dimensions={1}, use_global_device_ids=true | all-gather | bytes 26112 | tf_op jit(solution)/shard_map/all_gather | solution.py:73
  33.7 17.7 %all_gather.9 = f32[3,2048]{1,0:T(4,128)S(1)} all-gather(f32[3,128]{1,0:T(4,128)} %param.9), channel_id=1, replica_groups=mesh['group'=2,'src'=16] {'src'}, dimensions={1}, use_global_device_ids=true | all-gather | bytes 26112 | tf_op jit(solution)/shard_map/all_gather | solution.py:74
  51.4 19.2 %all_gather.11 = f32[8,2048]{1,0:T(8,128)S(1)} all-gather(f32[8,128]{1,0:T(8,128)} %param.10), channel_id=1, replica_groups=mesh['group'=2,'src'=16] {'src'}, dimensions={1}, use_global_device_ids=true | all-gather | bytes 69632 | tf_op jit(solution)/shard_map/all_gather | solution.py:75
  70.6 0.7 fusion.24
  71.3 0.0 collective-permute-done
  71.3 0.8 pad_maximum_fusion.1
  72.1 0.1 copy.26
  72.2 0.6 gather_fusion.1
  72.9 0.1 copy.29
  72.9 0.7 gather_fusion
  73.6 0.1 copy.27
  73.7 0.8 fusion.15
  74.5 0.0 copy-start.2
  74.5 0.0 copy-start.3
  74.6 0.3 multiply_divide_fusion.1
  74.9 0.3 multiply_divide_fusion.2
  75.3 0.0 copy-done.2
  75.3 0.0 copy-done.3
  75.3 1.8 %divide_multiply_fusion.1 = (f32[128,2048]{1,0:T(8,128)S(1)}, f32[128,2048]{1,0:T(8,128)S(1)}, f32[128,2048]{1,0:T(8,128)S(1)}, f32[128,2048]{1,0:T(8,128)S(1)},...) fusion(f32[128]{0:T(128)S(1)} %add_multiply_fusion.2, f32[2048]{0:T(1024)S(1)} %bitcast.136, ...), kind=kOutput, calls=%fused_computation.109 | convolution fusion | flops 31196160 | bytes 13726240 | tf_op jit(solution)/shard_map/while/body/eval_jaxpr/mj,mi->ji/dot_general | solution.py:85
  77.1 2.5 %multiply_reduce_fusion = (f32[3,128]{1,0:T(4,128)S(1)}, f32[128,2048]{1,0:T(8,128)S(1)}, f32[128,2048]{1,0:T(8,128)S(1)}, f32[128,2048]{1,0:T(8,128)S(1)}) fusion(f32[128,2048]{1,0:T(8,128)S(1)} %get-tuple-element.62, f32[128,2048]{1,0:T(8,128)S(1)} %get-tuple-element.92, f32[3,128]{1,0:T(4,128)S(1)} %bitcast.127, f32[128,2048]{1,0:T(8,128)S(1)} %get-tuple-element.94, ...), kind=kLoop, calls=%fused_computation.36 | loop fusion | flops 12582528 | bytes 8419328 | tf_op jit(solution)/shard_map/while/body/eval_jaxpr/transpose(jvp())/reduce_sum | solution.py:35
  79.6 0.2 multiply_multiply_fusion.3
  79.8 0.2 multiply_multiply_fusion.1
  80.1 0.6 fusion.28
  80.6 2.0 %multiply_bitcast_fusion.5 = (f32[1,128,2048]{2,1,0:T(8,128)}, f32[128,2048]{1,0:T(8,128)}, f32[128,2048]{1,0:T(8,128)S(1)}) fusion(f32[3,128,2048]{2,1,0:T(8,128)S(1)} %get-tuple-element.95, f32[128,2048]{1,0:T(8,128)S(1)} %get-tuple-element.67, f32[128,2048]{1,0:T(8,128)S(1)} %get-tuple-element.54, f32[2048]{0:T(1024)S(1)} %broadcast_multiply_fusion.2, ...), kind=kLoop, calls=%fused_computation.57 | loop fusion | flops 2359296 | bytes 9445376 | tf_op jit(solution)/shard_map/while/body/eval_jaxpr/transpose(jvp())/broadcast_in_dim | solution.py:31
  82.6 2.2 %multiply_bitcast_fusion.3 = (f32[1,128,2048]{2,1,0:T(8,128)S(1)}, f32[128,2048]{1,0:T(8,128)}, f32[1,128,2048]{2,1,0:T(8,128)S(1)}, f32[128,2048]{1,0:T(8,128)}...) fusion(f32[3,128,2048]{2,1,0:T(8,128)S(1)} %get-tuple-element.95, f32[128,2048]{1,0:T(8,128)S(1)} %get-tuple-element.66, ...), kind=kLoop, calls=%fused_computation.55 | loop fusion | flops 5236736 | bytes 11575296 | tf_op jit(solution)/shard_map/while/body/eval_jaxpr/transpose(jvp())/broadcast_in_dim | solution.py:30
  84.9 4.8 %multiply_bitcast_fusion.11 = (f32[1,128,2048]{2,1,0:T(8,128)S(1)}, f32[1,128,2048]{2,1,0:T(8,128)S(1)}, f32[1,128,2048]{2,1,0:T(8,128)S(1)}, f32[1,128,2048]{2,...) fusion(f32[128,2048]{1,0:T(8,128)} %get-tuple-element.56, ...), kind=kLoop, calls=%fused_computation.65 | loop fusion | flops 3145728 | bytes 18874368 | tf_op jit(solution)/shard_map/while/body/eval_jaxpr/transpose(jvp())/broadcast_in_dim | solution.py:31
  89.7 0.0 copy-start
  89.7 3.4 %fusion.27 = (f32[3,128]{1,0:T(4,128)S(1)}, f32[3,2048]{1,0:T(4,128)S(1)}) fusion(f32[1,128,2048]{2,1,0:T(8,128)} %get-tuple-element.88, f32[1,128,2048]{2,1,0:T(8,128)S(1)} %get-tuple-element.70, f32[1,128,2048]{2,1,0:T(8,128)} %get-tuple-element.89, f32[1,128,2048]{2,1,0:T(8,128)S(1)} %get-tuple-element.58, f32[1,128,2048]{2,1,0:T(8,128)} %get-tuple-element.90, ...), kind=kLoop, calls=%fused_computation.111 | loop fusion | flops 11003520 | bytes 9490944 | tf_op jit(solution)/shard_map/while/body/eval_jaxpr/transpose(jvp())/reduce_sum | solution.py:26
  93.1 0.0 copy-done
  93.1 0.0 copy-start.1
  93.1 1.9 %fusion.26 = (f32[3,128]{1,0:T(4,128)S(1)}, f32[3,2048]{1,0:T(4,128)S(1)}) fusion(f32[1,128,2048]{2,1,0:T(8,128)S(1)} %get-tuple-element.84, f32[1,128,2048]{2,1,0:T(8,128)S(1)} %get-tuple-element.85, f32[1,128,2048]{2,1,0:T(8,128)S(1)} %get-tuple-element.86, f32[1,128,2048]{2,1,0:T(8,128)S(1)} %copy-done, f32[1,128,2048]{2,1,0:T(8,128)S(1)} %get-tuple-element.73, ...), kind=kLoop, calls=%fused_computation.110 | loop fusion | flops 11789952 | bytes 9490944 | tf_op jit(solution)/shard_map/while/body/eval_jaxpr/transpose(jvp())/reduce_sum | solution.py:27
  95.0 0.1 copy.31
  95.1 0.1 copy.30
  95.2 1.0 scatter_custom_fusion
  96.2 1.2 scatter_fusion
  97.5 0.0 copy-done.1
  97.5 0.1 add_multiply_fusion.1
  97.6 0.6 pad_maximum_fusion
  98.2 0.0 reduce-scatter.2.cloned.1.call-update
  98.3 2.2 %collective-permute-start.1 = (f32[3,1]{0,1:T(1,128)S(1)}, f32[3,1]{0,1:T(1,128)S(1)}, u32[]{:S(2)}, u32[]{:S(2)}) collective-permute-start(f32[3,1]{0,1:T(1,128)S(1)} %slice.108), channel_id=1, source_target_pairs={{0,1},{1,2},{2,3},{3,4},{4,5},{5,6},{6,7},{7,8},{8,9},{9,10},{10,1... | collective-permute-start | bytes 44 | tf_op jit(solution)/shard_map/ppermute | solution.py:14
  100.5 0.1 copy.33
  100.6 0.7 collective-permute-done.1
  101.3 0.1 copy.32
  101.4 0.7 maximum_multiply_fusion
  102.1 45.5 %reduce-scatter.2.cloned.1.call-done = f32[6,128]{1,0:T(8,128)} async-done(((f32[6,2048]{1,0:T(8,128)}), f32[6,128]{1,0:T(8,128)}) %reduce-scatter.2.cloned.1.call-update) | async-done | bytes 3088 | tf_op jit(solution)/shard_map/reduce_scatter | solution.py:94
  (16 shorter events, 0.2 us)
Async XLA Ops:
  7.2 140.4 %reduce-scatter.2.cloned.1.call-start = ((), (), s32[]{:S(2)}) async-start(), calls=%async_computation.1 | async-start | bytes 69632 | tf_op jit(solution)/shard_map/reduce_scatter | solution.py:94
  7.2 64.1 %collective-permute-start = (f32[3,1]{1,0:T(4,128)}, f32[3,1]{1,0:T(4,128)S(1)}, u32[]{:S(2)}, u32[]{:S(2)}) collective-permute-start(f32[3,1]{1,0:T(4,128)} %bitcast.141), channel_id=1, source_target_pairs={{1,0},{2,1},{3,2},{4,3},{5,4},{6,5},{7,6},{8,7},{9,8},{10,9},{11,1... | collective-permute-start | bytes 44 | tf_op jit(solution)/shard_map/ppermute | solution.py:14
  74.5 0.7 copy-start.2
  74.5 0.7 copy-start.3
  89.7 3.4 %copy-start = (f32[1,128,2048]{2,1,0:T(8,128)S(1)}, f32[1,128,2048]{2,1,0:T(8,128)}, u32[]{:S(2)}) copy-start(f32[1,128,2048]{2,1,0:T(8,128)} %get-tuple-element.87) | copy-start | bytes 3145732
  93.1 4.4 %copy-start.1 = (f32[3]{0:T(128)S(1)}, f32[3]{0:T(128)}, u32[]{:S(2)}) copy-start(f32[3]{0:T(128)} %constant.34.clone) | copy-start | bytes 40
  98.3 3.1 %collective-permute-start.1 = (f32[3,1]{0,1:T(1,128)S(1)}, f32[3,1]{0,1:T(1,128)S(1)}, u32[]{:S(2)}, u32[]{:S(2)}) collective-permute-start(f32[3,1]{0,1:T(1,128)S(1)} %slice.108), channel_id=1, source_target_pairs={{0,1},{1,2},{2,3},{3,4},{4,5},{5,6},{6,7},{7,8},{8,9},{9,10},{10,1... | collective-permute-start | bytes 44 | tf_op jit(solution)/shard_map/ppermute | solution.py:14
Sparse Core Ops, SparseCore 0:
  98.4 49.1 reduce-scatter.1
where the time goes:
time: 155 us; the launch traced here: 154 us
  blocking collectives  60.7 us (39%)
  waiting for transfers between devices  46.3 us (30%)
  other arithmetic  25.1 us (16%)
  between operations  14.3 us (9%)
  starting transfers between devices  3.57 us (2%)
  local copies, waits for them, and re-layouts  2.68 us (2%)
  matrix products  1.85 us (1%)
    reduce_scatter x1, waiting for transfers between devices, on_device(): lax.psum_scatter(receiver_buffer, 'src', scatter_dimension=1, tiled=True)  45.5 us
    all_gather x1, blocking collectives, on_device(): shard_points = lax.all_gather(points, 'src', axis=1, tiled=True)  23.8 us
    all_gather x1, blocking collectives, on_device(): shard_left = lax.all_gather(left_modes, 'src', axis=1, tiled=True)  19.2 us
    all_gather x1, blocking collectives, on_device(): shard_normals = lax.all_gather(rcv_normals, 'src', axis=1, tiled=True)  17.7 us
    broadcast_in_dim x2, other arithmetic, tile_energy(): cross_z = rel_first[0] * rel_second[1] - rel_first[1] * rel_second[0]  6.79 us
    ppermute x2, starting transfers between devices, shifted(): lax.ppermute(value, axis, [(source, source + steps) for source in range(l...  3.54 us
    reduce_sum x1, other arithmetic, tile_energy(): rel_first = points[:, None, :] - first_end[:, :, None]  3.41 us
  transfers between devices with their start and end apart: 3, of which 2 were waited for; matrix products, arithmetic and copies ran while one was open for 2% of the time, Pallas kernels for 0%

commit v1 on v0

--- a/solution.py
+++ b/solution.py
@@ -70,7 +70,15 @@
         jnp.zeros((3, source_count), jnp.float32),
         jnp.zeros((6, receiver_count), jnp.float32),
     )
-    shard_points = lax.all_gather(points, "src", axis=1, tiled=True)
+    ways, here = (lax.axis_size("src"), lax.axis_index("src"))
+    grown, reach = (points, 1)
+    while reach < ways:
+        theirs = lax.ppermute(grown, "src", [(d, d ^ reach) for d in range(ways)])
+        mine_first = jnp.concatenate([grown, theirs], axis=1)
+        theirs_first = jnp.concatenate([theirs, grown], axis=1)
+        grown = jnp.where(here & reach == 0, mine_first, theirs_first)
+        reach = 2 * reach
+    shard_points = grown
     shard_normals = lax.all_gather(rcv_normals, "src", axis=1, tiled=True)
     shard_left = lax.all_gather(left_modes, "src", axis=1, tiled=True)
     row_count = shard_points.shape[1]

time: 155 us -> 148 us (0.955)
  blocking collectives: 60.7 us -> 42.1 us
  waiting for transfers between devices: 46.3 us -> 57 us
    all_gather x1 -> x0, blocking collectives: 23.8 us -> none  [on_device(): shard_points = lax.all_gather(points, 'src', axis=1, tiled=True)]
    ppermute x0 -> x4, waiting for transfers between devices: none -> 8.68 us  [on_device(): theirs = lax.ppermute(grown, 'src', [(d, d ^ reach) for d in range(ways)])]
    all_gather x1, blocking collectives: 17.7 us -> 24.2 us  [on_device(): shard_normals = lax.all_gather(rcv_normals, 'src', axis=1, tiled=True)]
    ppermute x0 -> x4, starting transfers between devices: none -> 2.14 us  [on_device(): theirs = lax.ppermute(grown, 'src', [(d, d ^ reach) for d in range(ways)])]
    reduce_scatter x1, waiting for transfers between devices: 45.5 us -> 47.5 us  [on_device(): lax.psum_scatter(receiver_buffer, 'src', scatter_dimension=1, tiled=True)]
  transfers between devices with their start and end apart: 3 -> 7, of which waited for: 2 -> 5; matrix products, arithmetic and copies ran while one was open for 2% -> 3% of each run, Pallas kernels for 0% -> 0%
where the time goes in v1:
time: 148 us
  waiting for transfers between devices  57 us (39%)
  blocking collectives  42.1 us (28%)
  other arithmetic  25.2 us (17%)
  between operations  14.3 us (10%)
  starting transfers between devices  4.75 us (3%)
  local copies, waits for them, and re-layouts  2.68 us (2%)
  matrix products  1.86 us (1%)
    reduce_scatter x1, waiting for transfers between devices, on_device(): lax.psum_scatter(receiver_buffer, 'src', scatter_dimension=1, tiled=True)  47.5 us
    all_gather x1, blocking collectives, on_device(): shard_normals = lax.all_gather(rcv_normals, 'src', axis=1, tiled=True)  24.2 us
    all_gather x1, blocking collectives, on_device(): shard_left = lax.all_gather(left_modes, 'src', axis=1, tiled=True)  17.9 us
    ppermute x4, waiting for transfers between devices, on_device(): theirs = lax.ppermute(grown, 'src', [(d, d ^ reach) for d in range(ways)])  8.68 us
    broadcast_in_dim x2, other arithmetic, tile_energy(): cross_z = rel_first[0] * rel_second[1] - rel_first[1] * rel_second[0]  6.79 us
    reduce_sum x1, other arithmetic, tile_energy(): rel_first = points[:, None, :] - first_end[:, :, None]  3.41 us
  transfers between devices with their start and end apart: 7, of which 5 were waited for; matrix products, arithmetic and copies ran while one was open for 3% of the time, Pallas kernels for 0%

profile of v1, /device:TPU:0, one launch (start us, length us, event | category | flops | bytes accessed | tf_op | source)
XLA Modules:
  0.0 147.8 jit_solution(16479198596927734575)
XLA Ops:
  7.2 0.0 reduce-scatter.2.cloned.1.call-start
  7.2 0.7 multiply_add_fusion.1
  7.9 0.7 slice.81
  8.6 0.5 collective-permute-start.1
  9.0 1.3 collective-permute-start
  10.3 24.2 %all_gather.6 = f32[3,2048]{1,0:T(4,128)S(1)} all-gather(f32[3,128]{1,0:T(4,128)} %param.9), channel_id=1, replica_groups=mesh['group'=2,'src'=16] {'src'}, dimensions={1}, use_global_device_ids=true | all-gather | bytes 26112 | tf_op jit(solution)/shard_map/all_gather | solution.py:82
  34.6 17.9 %all_gather.7 = f32[8,2048]{1,0:T(8,128)S(1)} all-gather(f32[8,128]{1,0:T(8,128)} %param.10), channel_id=1, replica_groups=mesh['group'=2,'src'=16] {'src'}, dimensions={1}, use_global_device_ids=true | all-gather | bytes 69632 | tf_op jit(solution)/shard_map/all_gather | solution.py:83
  52.5 0.7 fusion.24
  53.2 0.0 collective-permute-done
  53.2 0.8 pad_maximum_fusion.1
  54.0 0.0 collective-permute-done.1
  54.0 1.7 %collective-permute-start.2 = (f32[3,256]{1,0:T(4,128)S(1)}, f32[3,256]{1,0:T(4,128)S(1)}, u32[]{:S(2)}, u32[]{:S(2)}) collective-permute-start(f32[3,256]{1,0:T(4,128)S(1)} %maximum_select_fusion.3), channel_id=1, source_target_pairs={{0,2},{1,3},{2,0},{3,1},{4,6},{5,7},{6,4},{7,5},{8,10},{9,11},{10,... | collective-permute-start | bytes 9224 | tf_op jit(solution)/shard_map/ppermute | solution.py:76
  55.7 0.1 copy.26
  55.8 0.6 gather_fusion.1
  56.4 0.1 copy.29
  56.5 0.7 gather_fusion
  57.2 0.1 copy.27
  57.2 0.4 collective-permute-done.2
  57.7 0.0 collective-permute-start.3
  57.7 3.6 %collective-permute-done.3 = f32[3,512]{1,0:T(4,128)S(1)} collective-permute-done((f32[3,512]{1,0:T(4,128)S(1)}, f32[3,512]{1,0:T(4,128)S(1)}, u32[]{:S(2)}, u32[]{:S(2)}) %collective-permute-start.3) | collective-permute-done | bytes 6176 | tf_op jit(solution)/shard_map/ppermute | solution.py:76
  61.3 0.0 collective-permute-start.4
  61.3 4.6 %collective-permute-done.4 = f32[3,1024]{1,0:T(4,128)S(1)} collective-permute-done((f32[3,1024]{1,0:T(4,128)S(1)}, f32[3,1024]{1,0:T(4,128)S(1)}, u32[]{:S(2)}, u32[]{:S(2)}) %collective-permute-start.4) | collective-permute-done | bytes 12320 | tf_op jit(solution)/shard_map/ppermute | solution.py:76
  66.0 0.8 fusion.15
  66.8 0.0 copy-start.2
  66.8 0.0 copy-start.3
  66.8 0.3 multiply_divide_fusion.1
  67.2 0.3 multiply_divide_fusion.2
  67.5 0.0 copy-done.2
  67.5 0.0 copy-done.3
  67.5 1.9 %divide_multiply_fusion.1 = (f32[128,2048]{1,0:T(8,128)S(1)}, f32[128,2048]{1,0:T(8,128)S(1)}, f32[128,2048]{1,0:T(8,128)S(1)}, f32[128,2048]{1,0:T(8,128)S(1)},...) fusion(f32[128]{0:T(128)S(1)} %add_multiply_fusion.2, f32[2048]{0:T(1024)S(1)} %bitcast.136, ...), kind=kOutput, calls=%fused_computation.113 | convolution fusion | flops 31196160 | bytes 13726240 | tf_op jit(solution)/shard_map/while/body/eval_jaxpr/mj,mi->ji/dot_general | solution.py:93
  69.4 2.5 %multiply_reduce_fusion = (f32[3,128]{1,0:T(4,128)S(1)}, f32[128,2048]{1,0:T(8,128)S(1)}, f32[128,2048]{1,0:T(8,128)S(1)}, f32[128,2048]{1,0:T(8,128)S(1)}) fusion(f32[128,2048]{1,0:T(8,128)S(1)} %get-tuple-element.62, f32[128,2048]{1,0:T(8,128)S(1)} %get-tuple-element.92, f32[3,128]{1,0:T(4,128)S(1)} %bitcast.127, f32[128,2048]{1,0:T(8,128)S(1)} %get-tuple-element.94, ...), kind=kLoop, calls=%fused_computation.36 | loop fusion | flops 12582528 | bytes 8419328 | tf_op jit(solution)/shard_map/while/body/eval_jaxpr/transpose(jvp())/reduce_sum | solution.py:35
  71.9 0.2 multiply_multiply_fusion.3
  72.1 0.2 multiply_multiply_fusion.1
  72.3 0.6 fusion.28
  72.9 2.0 %multiply_bitcast_fusion.5 = (f32[1,128,2048]{2,1,0:T(8,128)}, f32[128,2048]{1,0:T(8,128)}, f32[128,2048]{1,0:T(8,128)S(1)}) fusion(f32[3,128,2048]{2,1,0:T(8,128)S(1)} %get-tuple-element.95, f32[128,2048]{1,0:T(8,128)S(1)} %get-tuple-element.67, f32[128,2048]{1,0:T(8,128)S(1)} %get-tuple-element.54, f32[2048]{0:T(1024)S(1)} %broadcast_multiply_fusion.2, ...), kind=kLoop, calls=%fused_computation.57 | loop fusion | flops 2359296 | bytes 9445376 | tf_op jit(solution)/shard_map/while/body/eval_jaxpr/transpose(jvp())/broadcast_in_dim | solution.py:31
  74.9 2.2 %multiply_bitcast_fusion.3 = (f32[1,128,2048]{2,1,0:T(8,128)S(1)}, f32[128,2048]{1,0:T(8,128)}, f32[1,128,2048]{2,1,0:T(8,128)S(1)}, f32[128,2048]{1,0:T(8,128)}...) fusion(f32[3,128,2048]{2,1,0:T(8,128)S(1)} %get-tuple-element.95, f32[128,2048]{1,0:T(8,128)S(1)} %get-tuple-element.66, ...), kind=kLoop, calls=%fused_computation.55 | loop fusion | flops 5236736 | bytes 11575296 | tf_op jit(solution)/shard_map/while/body/eval_jaxpr/transpose(jvp())/broadcast_in_dim | solution.py:30
  77.1 4.8 %multiply_bitcast_fusion.11 = (f32[1,128,2048]{2,1,0:T(8,128)S(1)}, f32[1,128,2048]{2,1,0:T(8,128)S(1)}, f32[1,128,2048]{2,1,0:T(8,128)S(1)}, f32[1,128,2048]{2,...) fusion(f32[128,2048]{1,0:T(8,128)} %get-tuple-element.56, ...), kind=kLoop, calls=%fused_computation.65 | loop fusion | flops 3145728 | bytes 18874368 | tf_op jit(solution)/shard_map/while/body/eval_jaxpr/transpose(jvp())/broadcast_in_dim | solution.py:31
  81.9 0.0 copy-start
  81.9 3.4 %fusion.27 = (f32[3,128]{1,0:T(4,128)S(1)}, f32[3,2048]{1,0:T(4,128)S(1)}) fusion(f32[1,128,2048]{2,1,0:T(8,128)} %get-tuple-element.88, f32[1,128,2048]{2,1,0:T(8,128)S(1)} %get-tuple-element.70, f32[1,128,2048]{2,1,0:T(8,128)} %get-tuple-element.89, f32[1,128,2048]{2,1,0:T(8,128)S(1)} %get-tuple-element.58, f32[1,128,2048]{2,1,0:T(8,128)} %get-tuple-element.90, ...), kind=kLoop, calls=%fused_computation.115 | loop fusion | flops 11003520 | bytes 9490944 | tf_op jit(solution)/shard_map/while/body/eval_jaxpr/transpose(jvp())/reduce_sum | solution.py:26
  85.4 0.0 copy-done
  85.4 0.0 copy-start.1
  85.4 1.9 %fusion.26 = (f32[3,128]{1,0:T(4,128)S(1)}, f32[3,2048]{1,0:T(4,128)S(1)}) fusion(f32[1,128,2048]{2,1,0:T(8,128)S(1)} %get-tuple-element.84, f32[1,128,2048]{2,1,0:T(8,128)S(1)} %get-tuple-element.85, f32[1,128,2048]{2,1,0:T(8,128)S(1)} %get-tuple-element.86, f32[1,128,2048]{2,1,0:T(8,128)S(1)} %copy-done, f32[1,128,2048]{2,1,0:T(8,128)S(1)} %get-tuple-element.73, ...), kind=kLoop, calls=%fused_computation.114 | loop fusion | flops 11789952 | bytes 9490944 | tf_op jit(solution)/shard_map/while/body/eval_jaxpr/transpose(jvp())/reduce_sum | solution.py:27
  87.3 0.1 copy.31
  87.4 0.1 copy.30
  87.5 1.0 scatter_custom_fusion
  88.5 1.2 scatter_fusion
  89.8 0.0 copy-done.1
  89.8 0.1 add_multiply_fusion.1
  89.9 0.6 pad_maximum_fusion
  90.5 0.0 reduce-scatter.2.cloned.1.call-update
  90.5 1.3 collective-permute-start.5
  91.8 0.1 copy.33
  91.9 0.7 collective-permute-done.5
  92.6 0.1 copy.32
  92.7 0.7 maximum_multiply_fusion
  93.4 47.5 %reduce-scatter.2.cloned.1.call-done = f32[6,128]{1,0:T(8,128)} async-done(((f32[6,2048]{1,0:T(8,128)}), f32[6,128]{1,0:T(8,128)}) %reduce-scatter.2.cloned.1.call-update) | async-done | bytes 3088 | tf_op jit(solution)/shard_map/reduce_scatter | solution.py:102
  (20 shorter events, 0.2 us)
Async XLA Ops:
  7.2 133.8 %reduce-scatter.2.cloned.1.call-start = ((), (), s32[]{:S(2)}) async-start(), calls=%async_computation.1 | async-start | bytes 69632 | tf_op jit(solution)/shard_map/reduce_scatter | solution.py:102
  8.6 45.4 %collective-permute-start.1 = (f32[3,128]{1,0:T(4,128)S(1)}, f32[3,128]{1,0:T(4,128)S(1)}, u32[]{:S(2)}, u32[]{:S(2)}) collective-permute-start(f32[3,128]{1,0:T(4,128)S(1)} %pad_maximum_fusion.3), channel_id=1, source_target_pairs={{0,1},{1,0},{2,3},{3,2},{4,5},{5,4},{6,7},{7,6},{8,9},{9,8},{10,11... | collective-permute-start | bytes 4616 | tf_op jit(solution)/shard_map/ppermute | solution.py:76
  9.0 44.1 %collective-permute-start = (f32[3,1]{1,0:T(4,128)}, f32[3,1]{1,0:T(4,128)S(1)}, u32[]{:S(2)}, u32[]{:S(2)}) collective-permute-start(f32[3,1]{1,0:T(4,128)} %bitcast.141), channel_id=1, source_target_pairs={{1,0},{2,1},{3,2},{4,3},{5,4},{6,5},{7,6},{8,7},{9,8},{10,9},{11,1... | collective-permute-start | bytes 44 | tf_op jit(solution)/shard_map/ppermute | solution.py:14
  54.0 3.7 %collective-permute-start.2 = (f32[3,256]{1,0:T(4,128)S(1)}, f32[3,256]{1,0:T(4,128)S(1)}, u32[]{:S(2)}, u32[]{:S(2)}) collective-permute-start(f32[3,256]{1,0:T(4,128)S(1)} %maximum_select_fusion.3), channel_id=1, source_target_pairs={{0,2},{1,3},{2,0},{3,1},{4,6},{5,7},{6,4},{7,5},{8,10},{9,11},{10,... | collective-permute-start | bytes 9224 | tf_op jit(solution)/shard_map/ppermute | solution.py:76
  57.7 3.7 %collective-permute-start.3 = (f32[3,512]{1,0:T(4,128)S(1)}, f32[3,512]{1,0:T(4,128)S(1)}, u32[]{:S(2)}, u32[]{:S(2)}) collective-permute-start(f32[3,512]{1,0:T(4,128)S(1)} %maximum_select_fusion.2), channel_id=1, source_target_pairs={{0,4},{1,5},{2,6},{3,7},{4,0},{5,1},{6,2},{7,3},{8,12},{9,13},{10,... | collective-permute-start | bytes 18440 | tf_op jit(solution)/shard_map/ppermute | solution.py:76
  61.3 4.6 %collective-permute-start.4 = (f32[3,1024]{1,0:T(4,128)S(1)}, f32[3,1024]{1,0:T(4,128)S(1)}, u32[]{:S(2)}, u32[]{:S(2)}) collective-permute-start(f32[3,1024]{1,0:T(4,128)S(1)} %maximum_select_fusion.1), channel_id=1, source_target_pairs={{0,8},{1,9},{2,10},{3,11},{4,12},{5,13},{6,14},{7,15},{8,0},{9,1},... | collective-permute-start | bytes 36872 | tf_op jit(solution)/shard_map/ppermute | solution.py:76
  66.8 0.7 copy-start.2
  66.8 0.7 copy-start.3
  81.9 3.4 %copy-start = (f32[1,128,2048]{2,1,0:T(8,128)S(1)}, f32[1,128,2048]{2,1,0:T(8,128)}, u32[]{:S(2)}) copy-start(f32[1,128,2048]{2,1,0:T(8,128)} %get-tuple-element.87) | copy-start | bytes 3145732
  85.4 4.4 %copy-start.1 = (f32[3]{0:T(128)S(1)}, f32[3]{0:T(128)}, u32[]{:S(2)}) copy-start(f32[3]{0:T(128)} %constant.15.clone) | copy-start | bytes 40
  90.5 2.1 %collective-permute-start.5 = (f32[3,1]{0,1:T(1,128)S(1)}, f32[3,1]{0,1:T(1,128)S(1)}, u32[]{:S(2)}, u32[]{:S(2)}) collective-permute-start(f32[3,1]{0,1:T(1,128)S(1)} %slice.108), channel_id=1, source_target_pairs={{0,1},{1,2},{2,3},{3,4},{4,5},{5,6},{6,7},{7,8},{8,9},{9,10},{10,1... | collective-permute-start | bytes 44 | tf_op jit(solution)/shard_map/ppermute | solution.py:14
Sparse Core Ops, SparseCore 0:
  90.7 50.2 reduce-scatter.1
